TPU v7x, 32 devices: a whole 2x2x4 slice. The times are simulated.
32 devices in a mesh: aux: 4 (over y, x), blk: 8 (over z, core).
Axes of the slice: x: 2, y: 2, z: 4, core: 2. Of those that a mesh axis runs over, the one named last changes fastest.
Arguments:
- three_center: bfloat16 [384, 4, 128, 128], P(('aux', 'blk')), may hold values from -6 to 6
- slot_block: int32 [384], P(('aux', 'blk')), may hold values from 0 to 47
- slot_aux: int32 [384], P(('aux', 'blk')), may hold values from 0 to 1
- live_slots: int32 [32], P(('aux', 'blk')), may hold values from 1 to 12, as said below
- vir_coef: bfloat16 [6144, 256], replicated, may hold values from -0.00478416 to 0.00478416
- eps_occ: float32 [4000], replicated, may hold values from -1.5 to -0.3
- eps_vir: float32 [256], replicated, may hold values from 0.2 to 3
- occ_index: int32 [4], replicated, may hold values from 0 to 3999, as said below
Outputs:
- amplitudes: float32 [4, 256, 4, 256], P('aux', 'blk')
- pair_energy: float32 [4, 4], P('aux')
Inputs may be any that keep to these rules, and one draw needn't show every extreme that they name: The slots in use on a device are its first live_slots ones; the others hold data that is not used. Some device holds exactly 12 slots in use in every draw. `occ_index`: the indices are distinct; the first and the last occupied orbital of the system are in every batch.
All inputs are finite; a program needn't handle non-finite values.
Results may differ from a plain program's by a relative error of at most 0.0035.
Values may be sent and summed in bfloat16 or wider, within the bound.
A program may use at most 64 MiB of HBM per device.

v0:
```python
import jax
import jax.numpy as jnp
from jax import lax
from jax.sharding import PartitionSpec as P

AUX_BLOCKS_DEV = 2


def body(three_center, slot_block, slot_aux, live_slots, vir_coef, eps_occ, eps_vir, occ_index):
    blk_count = lax.axis_size("blk")
    occ_row = lax.axis_index("aux")
    slot_count = three_center.shape[0]
    occ_count = three_center.shape[1]
    ao_span = three_center.shape[3]
    vir_count = vir_coef.shape[1]
    coef_blocks = vir_coef.reshape(vir_coef.shape[0] // ao_span, ao_span, vir_count)
    coefficients = jnp.take(coef_blocks, slot_block, axis=0)
    products = jnp.einsum(
        "soqn,snv->soqv", three_center, coefficients, preferred_element_type=jnp.float32
    )
    keep = (jnp.arange(slot_count) < live_slots[0]).astype(jnp.float32)
    select = (slot_aux[:, None] == jnp.arange(AUX_BLOCKS_DEV)[None, :]).astype(jnp.float32)
    select = select * keep[:, None]
    local_rows = jnp.einsum("sk,soqv->kqov", select, products).astype(jnp.bfloat16)
    halfed = lax.all_gather(local_rows, "aux", axis=0, tiled=True)
    own_rows = lax.dynamic_index_in_dim(halfed, occ_row, 2, keepdims=False)
    rows_dev = vir_count // blk_count
    mixed = lax.dot_general(
        halfed, own_rows, (((0, 1), (0, 1)), ((), ())), preferred_element_type=jnp.float32
    )
    summed = lax.psum_scatter(
        jnp.stack(
            [
                lax.dot_general(
                    own_rows,
                    halfed,
                    (((0, 1), (0, 1)), ((), ())),
                    preferred_element_type=jnp.float32,
                ),
                jnp.transpose(mixed, (1, 0, 2)),
            ],
            axis=1,
        ),
        "blk",
        scatter_dimension=0,
        tiled=True,
    )
    direct = summed[:, 0]
    crossed = summed[:, 1]
    first_vir = lax.axis_index("blk") * rows_dev
    occ_levels = jnp.take(eps_occ, occ_index)
    own_level = jnp.sum(jnp.where(jnp.arange(occ_count) == occ_row, occ_levels, 0.0))
    vir_levels = lax.dynamic_slice_in_dim(eps_vir, first_vir, rows_dev, 0)
    denominator = (
        own_level + occ_levels[None, :, None] - vir_levels[:, None, None] - eps_vir[None, None, :]
    )
    amplitudes = (direct / denominator)[None]
    pair_part = jnp.sum(direct * (2.0 * direct - crossed) / denominator, axis=(0, 2))
    pair_energy = lax.psum(pair_part, "blk")[None]
    return (amplitudes, pair_energy)


def solution(mesh):
    in_specs = (
        P(("aux", "blk"), None, None, None),
        P(("aux", "blk")),
        P(("aux", "blk")),
        P(("aux", "blk")),
        P(),
        P(),
        P(),
        P(),
    )
    out_specs = (P("aux", "blk", None, None), P("aux", None))
    return jax.shard_map(body, mesh=mesh, in_specs=in_specs, out_specs=out_specs, check_vma=False)
```

profile of v0, /device:TPU:0, one launch (start us, length us, event | category | flops | bytes accessed | tf_op | source)
XLA Modules:
  0.0 131.5 jit_solution(10336060481008152967)
XLA Ops:
  7.2 0.8 compare_select_fusion.1
  8.0 0.8 compare_and_fusion
  8.8 0.3 copy-done
  9.1 1.5 %gather_fusion = bf16[12,128,256]{2,1,0:T(8,128)(2,1)} fusion(bf16[48,128,256]{2,1,0:T(8,128)(2,1)S(1)} %bitcast.68, s32[1024]{0:T(1024)S(1)} %pad_clamp_fusion.1), kind=kCustom, calls=%fused_computation | custom fusion | bytes 1572912 | tf_op jit(solution)/shard_map/jit(_take)/gather | solution.py:17
  10.6 4.8 %convolution_bitcast_fusion = bf16[12,4,128,256]{2,3,1,0:T(8,128)(2,1)} fusion(bf16[12,4,128,128]{3,2,1,0:T(8,128)(2,1)} %param.8, bf16[12,128,256]{2,1,0:T(8,128)(2,1)} %gather_fusion, pred[12]{0:T(512)(128)(4,1)S(1)} %compare_and_fusion), kind=kOutput, calls=%fused_computation.2 | convolution fusion | flops 403046400 | bytes 5505036 | tf_op jit(solution)/shard_map/soqn,snv->soqv/dot_general | solution.py:18
  15.4 7.7 %copy.28 = bf16[12,4,128,256]{3,0,2,1:T(8,128)(2,1)} copy(bf16[12,4,128,256]{2,3,1,0:T(8,128)(2,1)} %convolution_bitcast_fusion) | data formatting | bytes 6291456 | tf_op jit(solution)/shard_map/soqn,snv->soqv/dot_general | solution.py:18
  23.7 2.9 %fusion = bf16[2,128,4,256]{3,0,1,2:T(2,128)(2,1)S(1)} fusion(bf16[12,4,128,256]{3,0,2,1:T(8,128)(2,1)} %copy.28, bf16[12]{0:T(256)(128)(2,1)S(1)} %compare_convert_fusion, s32[12]{0:T(128)S(1)} %copy-done.4), kind=kOutput, calls=%fused_computation.7 | convolution fusion | flops 6291504 | bytes 3670088 | tf_op jit(solution)/shard_map/sk,soqv->kqov/dot_general | solution.py:24
  26.6 0.9 copy.29
  27.5 0.0 reduce-scatter.2.cloned.1.call-start
  27.6 38.0 %all-gather.2.cloned.1.call-done = bf16[8,128,4,256]{3,1,2,0:T(8,128)(2,1)} async-done(((bf16[2,128,4,256]{3,1,2,0:T(8,128)(2,1)}), bf16[8,128,4,256]{3,1,2,0:T(8,128)(2,1)}) %all-gather.2.cloned.1.call-update) | async-done | bytes 2097168 | tf_op jit(solution)/shard_map/all_gather | solution.py:25
  65.6 2.6 %convolution_bitcast_fusion.2 = f32[256,1,4,256]{3,0,2,1:T(8,128)S(1)} fusion(bf16[8,128,4,256]{3,1,2,0:T(8,128)(2,1)} %all-gather.2.cloned.1.call-done, s32[]{:T(128)S(6)} %select_n.33), kind=kOutput, calls=%fused_computation.5 | convolution fusion | flops 536870912 | bytes 3670020 | tf_op jit(solution)/shard_map/dot_general | solution.py:28
  68.2 0.7 convolution_bitcast_fusion.1
  68.9 1.5 %pad_maximum_fusion = f32[256,2,4,256]{3,0,2,1:T(8,128)} fusion(f32[256,1,4,256]{3,0,2,1:T(8,128)S(1)} %convolution_bitcast_fusion.2, f32[256,1,4,256]{3,0,2,1:T(8,128)S(1)} %convolution_bitcast_fusion.1), kind=kLoop, calls=%fused_computation.3 | loop fusion | flops 524288 | bytes 4194304 | tf_op jit(solution)/shard_map/stack | solution.py:32
  70.4 0.6 copy-done.2
  71.1 0.1 dynamic_slice.8
  71.2 0.6 gather_fusion.1
  71.8 0.6 fusion.16
  72.4 0.7 broadcast_add_fusion
  73.1 0.1 broadcast_subtract_fusion
  73.2 33.5 %reduce-scatter.2.cloned.1.call-done = f32[32,2,4,256]{3,0,2,1:T(8,128)} async-done(((f32[256,2,4,256]{3,0,2,1:T(8,128)}), f32[32,2,4,256]{3,0,2,1:T(8,128)}) %reduce-scatter.2.cloned.1.call-update) | async-done | bytes 262160 | tf_op jit(solution)/shard_map/reduce_scatter | solution.py:31
  106.7 1.0 bitcast_divide_fusion
  107.7 0.7 copy.34
  108.4 1.2 fusion.12
  109.6 15.1 %psum.7 = f32[1,4]{1,0:T(1,128)} all-reduce(f32[1,4]{1,0:T(1,128)S(1)} %bitcast.69), channel_id=1, replica_groups=mesh['aux'=4,'blk'=8] {'blk'}, use_global_device_ids=true, to_apply=%region_3.4 | all-reduce | flops 4 | bytes 32 | tf_op jit(solution)/shard_map/psum | solution.py:59
  (17 shorter events, 0.1 us)
Async XLA Ops:
  7.2 1.9 %copy-start = (bf16[6144,256]{1,0:T(8,128)(2,1)S(1)}, bf16[6144,256]{1,0:T(8,128)(2,1)}, u32[]{:S(2)}) copy-start(bf16[6144,256]{1,0:T(8,128)(2,1)} %param.12) | copy-start | bytes 9437188
  7.2 58.4 %all-gather.2.cloned.1.call-start = ((), (), s32[]{:S(2)}) async-start(), calls=%async_computation.1 | async-start | bytes 2621440 | tf_op jit(solution)/shard_map/all_gather | solution.py:25
  15.4 8.4 %copy-start.4 = (s32[12]{0:T(128)S(1)}, s32[12]{0:T(128)}, u32[]{:S(2)}) copy-start(s32[12]{0:T(128)} %param.10) | copy-start | bytes 148
  27.5 79.1 %reduce-scatter.2.cloned.1.call-start = ((), (), s32[]{:S(2)}) async-start(), calls=%async_computation.2 | async-start | bytes 2359296 | tf_op jit(solution)/shard_map/reduce_scatter | solution.py:31
  65.6 2.6 %copy-start.5 = (bf16[8,128,4,256]{3,1,2,0:T(8,128)(2,1)S(1)}, bf16[8,128,4,256]{3,1,2,0:T(8,128)(2,1)}, u32[]{:S(2)}) copy-start(bf16[8,128,4,256]{3,1,2,0:T(8,128)(2,1)} %all-gather.2.cloned.1.call-done) | copy-start | bytes 6291460
  70.4 0.7 copy-start.2
  70.4 0.8 copy-start.3
  70.4 0.8 copy-start.1
Sparse Core Ops, SparseCore 0:
  27.6 37.8 all-gather.1
  70.6 36.0 reduce-scatter.1
where the time goes:
time: 132 us; the launch traced here: 131 us
  waiting for transfers between devices  71.6 us (54%)
  blocking collectives  15.1 us (11%)
  between operations  14.8 us (11%)
  local copies, waits for them, and re-layouts  12.5 us (9%)
  matrix products  11 us (8%)
  other arithmetic  6.57 us (5%)
    all_gather x1, waiting for transfers between devices, body(): halfed = lax.all_gather(local_rows, 'aux', axis=0, tiled=True)  38 us
    reduce_scatter x1, waiting for transfers between devices, body(): lax.psum_scatter(jnp.stack([lax.dot_general(own_rows, halfed, (((0, 1), (...  33.5 us
    psum x1, blocking collectives, body(): pair_energy = lax.psum(pair_part, 'blk')[None]  15.1 us
    dot_general x1, local copies, waits for them, and re-layouts, body(): jnp.einsum('soqn,snv->soqv', three_center, coefficients, preferred_elemen...  7.69 us
    dot_general x1, matrix products, body(): jnp.einsum('soqn,snv->soqv', three_center, coefficients, preferred_elemen...  4.8 us
    dot_general x1, matrix products, body(): jnp.einsum('sk,soqv->kqov', select, products).astype(jnp.bfloat16)  2.88 us
  transfers between devices with their start and end apart: 2, of which 2 were waited for; matrix products, arithmetic and copies ran while one was open for 2% of the time, Pallas kernels for 0%

commit v1 on v0

--- a/solution.py
+++ b/solution.py
@@ -22,7 +22,12 @@
     select = (slot_aux[:, None] == jnp.arange(AUX_BLOCKS_DEV)[None, :]).astype(jnp.float32)
     select = select * keep[:, None]
     local_rows = jnp.einsum("sk,soqv->kqov", select, products).astype(jnp.bfloat16)
-    halfed = lax.all_gather(local_rows, "aux", axis=0, tiled=True)
+    queue = []
+    for _ in range(jax.lax.axis_size("aux")):
+        queue.append(local_rows)
+    y = jnp.stack(queue, axis=0)
+    latest = jax.lax.all_to_all(y, axis_name="aux", split_axis=0, concat_axis=0)
+    halfed = jnp.concatenate(latest, axis=0)
     own_rows = lax.dynamic_index_in_dim(halfed, occ_row, 2, keepdims=False)
     rows_dev = vir_count // blk_count
     mixed = lax.dot_general(

time: 132 us -> 126 us (0.955)
  waiting for transfers between devices: 71.6 us -> 59.7 us
  starting transfers between devices: 0.08 us -> 5.19 us
  local copies, waits for them, and re-layouts: 12.5 us -> 14.9 us
  matrix products: 11 us -> 9.16 us
    all_gather x1 -> x0, waiting for transfers between devices: 38 us -> none  [body(): halfed = lax.all_gather(local_rows, 'aux', axis=0, tiled=True)]
    all_to_all x0 -> x1, waiting for transfers between devices: none -> 25.7 us  [body(): latest = jax.lax.all_to_all(y, axis_name='aux', split_axis=0, concat_axis=0)]
    all_to_all x0 -> x1, starting transfers between devices: none -> 5.19 us  [body(): latest = jax.lax.all_to_all(y, axis_name='aux', split_axis=0, concat_axis=0)]
    dot_general x1, matrix products: 2.57 us -> 0.74 us  [body(): lax.dot_general(halfed, own_rows, (((0, 1), (0, 1)), ((), ())), preferred...]
    all_to_all x0 -> x1, local copies, waits for them, and re-layouts: none -> 1.73 us  [body(): latest = jax.lax.all_to_all(y, axis_name='aux', split_axis=0, concat_axis=0)]
    another operation x0 -> x1, local copies, waits for them, and re-layouts: none -> 1.53 us  [body(): y = jnp.stack(queue, axis=0)]
where the time goes in v1:
time: 126 us
  waiting for transfers between devices  59.7 us (47%)
  blocking collectives  15.2 us (12%)
  local copies, waits for them, and re-layouts  14.9 us (12%)
  between operations  14.8 us (12%)
  matrix products  9.16 us (7%)
  other arithmetic  6.62 us (5%)
  starting transfers between devices  5.19 us (4%)
    reduce_scatter x1, waiting for transfers between devices, body(): lax.psum_scatter(jnp.stack([lax.dot_general(own_rows, halfed, (((0, 1), (...  34 us
    all_to_all x1, waiting for transfers between devices, body(): latest = jax.lax.all_to_all(y, axis_name='aux', split_axis=0, concat_axis=0)  25.7 us
    psum x1, blocking collectives, body(): pair_energy = lax.psum(pair_part, 'blk')[None]  15.2 us
    dot_general x1, local copies, waits for them, and re-layouts, body(): jnp.einsum('soqn,snv->soqv', three_center, coefficients, preferred_elemen...  7.7 us
    all_to_all x1, starting transfers between devices, body(): latest = jax.lax.all_to_all(y, axis_name='aux', split_axis=0, concat_axis=0)  5.19 us
    dot_general x1, matrix products, body(): jnp.einsum('soqn,snv->soqv', three_center, coefficients, preferred_elemen...  4.8 us
    dot_general x1, matrix products, body(): jnp.einsum('sk,soqv->kqov', select, products).astype(jnp.bfloat16)  2.88 us
  transfers between devices with their start and end apart: 2, of which 2 were waited for; matrix products, arithmetic and copies ran while one was open for 2% of the time, Pallas kernels for 0%

profile of v1, /device:TPU:0, one launch (start us, length us, event | category | flops | bytes accessed | tf_op | source)
XLA Modules:
  0.0 125.5 jit_solution(9324164239250035023)
XLA Ops:
  7.2 0.8 compare_select_fusion.1
  8.0 0.8 compare_and_fusion
  8.8 0.3 copy-done
  9.1 1.5 %gather_fusion = bf16[12,128,256]{2,1,0:T(8,128)(2,1)} fusion(bf16[48,128,256]{2,1,0:T(8,128)(2,1)S(1)} %bitcast.61, s32[1024]{0:T(1024)S(1)} %pad_clamp_fusion.1), kind=kCustom, calls=%fused_computation | custom fusion | bytes 1572912 | tf_op jit(solution)/shard_map/jit(_take)/gather | solution.py:17
  10.6 4.8 %convolution_bitcast_fusion = bf16[12,4,128,256]{2,3,1,0:T(8,128)(2,1)} fusion(bf16[12,4,128,128]{3,2,1,0:T(8,128)(2,1)} %param.8, bf16[12,128,256]{2,1,0:T(8,128)(2,1)} %gather_fusion, pred[12]{0:T(512)(128)(4,1)S(1)} %compare_and_fusion), kind=kOutput, calls=%fused_computation.2 | convolution fusion | flops 403046400 | bytes 5505036 | tf_op jit(solution)/shard_map/soqn,snv->soqv/dot_general | solution.py:18
  15.4 7.7 %copy.25 = bf16[12,4,128,256]{3,0,2,1:T(8,128)(2,1)} copy(bf16[12,4,128,256]{2,3,1,0:T(8,128)(2,1)} %convolution_bitcast_fusion) | data formatting | bytes 6291456 | tf_op jit(solution)/shard_map/soqn,snv->soqv/dot_general | solution.py:18
  23.7 2.9 %fusion = bf16[2,128,4,256]{3,0,1,2:T(2,128)(2,1)S(1)} fusion(bf16[12,4,128,256]{3,0,2,1:T(8,128)(2,1)} %copy.25, bf16[12]{0:T(256)(128)(2,1)S(1)} %compare_convert_fusion, s32[12]{0:T(128)S(1)} %copy-done.4), kind=kOutput, calls=%fused_computation.7 | convolution fusion | flops 6291504 | bytes 3670088 | tf_op jit(solution)/shard_map/sk,soqv->kqov/dot_general | solution.py:24
  26.6 0.1 copy.26
  26.7 1.5 %stack.16 = bf16[4,2,128,4,256]{4,2,1,3,0:T(8,128)(2,1)} broadcast(bf16[2,128,4,256]{3,1,0,2:T(8,128)(2,1)S(1)} %copy.26), dimensions={1,2,3,4} | broadcast | bytes 2621440 | tf_op jit(solution)/shard_map/stack | solution.py:28
  28.3 5.2 %all-to-all-start = ((bf16[4,2,128,4,256]{4,2,1,3,0:T(8,128)(2,1)}), bf16[4,2,128,4,256]{4,2,1,3,0:T(8,128)(2,1)}, u32[]{:S(2)}, u32[]{:S(2)}) async-start(bf16[4,2,128,4,256]{4,2,1,3,0:T(8,128)(2,1)} %stack.16), calls=%async_computation | async-start | bytes 4194304 | tf_op jit(solution)/shard_map/all_to_all | solution.py:29
  33.4 25.7 %all-to-all-done = bf16[4,2,128,4,256]{4,2,1,3,0:T(8,128)(2,1)} async-done(((bf16[4,2,128,4,256]{4,2,1,3,0:T(8,128)(2,1)}), bf16[4,2,128,4,256]{4,2,1,3,0:T(8,128)(2,1)}, u32[]{:S(2)}, u32[]{:S(2)}) %all-to-all-start) | async-done | bytes 2097184 | tf_op jit(solution)/shard_map/all_to_all | solution.py:29
  59.2 1.7 %copy.27 = bf16[4,2,128,4,256]{4,2,1,0,3:T(8,128)(2,1)S(1)} copy(bf16[4,2,128,4,256]{4,2,1,3,0:T(8,128)(2,1)} %all-to-all-done) | data formatting | bytes 4194304 | tf_op jit(solution)/shard_map/all_to_all | solution.py:29
  60.9 0.7 convolution_bitcast_fusion.1
  61.7 0.7 convolution_bitcast_fusion.2
  62.4 1.5 %pad_maximum_fusion = f32[256,2,4,256]{3,0,2,1:T(8,128)} fusion(f32[256,1,4,256]{3,0,2,1:T(8,128)S(1)} %convolution_bitcast_fusion.1, f32[256,1,4,256]{3,0,2,1:T(8,128)S(1)} %convolution_bitcast_fusion.2), kind=kLoop, calls=%fused_computation.3 | loop fusion | flops 524288 | bytes 4194304 | tf_op jit(solution)/shard_map/stack | solution.py:37
  63.9 0.6 copy-done.2
  64.7 0.6 gather_fusion.1
  65.3 0.6 fusion.16
  65.9 0.7 broadcast_add_fusion
  66.6 34.0 %reduce-scatter.2.cloned.1.call-done = f32[32,2,4,256]{3,0,2,1:T(8,128)} async-done(((f32[256,2,4,256]{3,0,2,1:T(8,128)}), f32[32,2,4,256]{3,0,2,1:T(8,128)}) %reduce-scatter.2.cloned.1.call-update) | async-done | bytes 262160 | tf_op jit(solution)/shard_map/reduce_scatter | solution.py:36
  100.6 1.0 bitcast_divide_fusion
  101.6 0.7 copy.30
  102.4 1.2 fusion.12
  103.5 15.2 %psum.7 = f32[1,4]{1,0:T(1,128)} all-reduce(f32[1,4]{1,0:T(1,128)S(1)} %bitcast.64), channel_id=1, replica_groups=mesh['aux'=4,'blk'=8] {'blk'}, use_global_device_ids=true, to_apply=%region_3.4 | all-reduce | flops 4 | bytes 32 | tf_op jit(solution)/shard_map/psum | solution.py:64
  (16 shorter events, 0.2 us)
Async XLA Ops:
  7.2 1.9 %copy-start = (bf16[6144,256]{1,0:T(8,128)(2,1)S(1)}, bf16[6144,256]{1,0:T(8,128)(2,1)}, u32[]{:S(2)}) copy-start(bf16[6144,256]{1,0:T(8,128)(2,1)} %param.12) | copy-start | bytes 9437188
  15.4 8.4 %copy-start.4 = (s32[12]{0:T(128)S(1)}, s32[12]{0:T(128)}, u32[]{:S(2)}) copy-start(s32[12]{0:T(128)} %param.10) | copy-start | bytes 148
  28.3 30.9 %all-to-all-start = ((bf16[4,2,128,4,256]{4,2,1,3,0:T(8,128)(2,1)}), bf16[4,2,128,4,256]{4,2,1,3,0:T(8,128)(2,1)}, u32[]{:S(2)}, u32[]{:S(2)}) async-start(bf16[4,2,128,4,256]{4,2,1,3,0:T(8,128)(2,1)} %stack.16), calls=%async_computation | async-start | bytes 4194304 | tf_op jit(solution)/shard_map/all_to_all | solution.py:29
  33.4 67.2 %reduce-scatter.2.cloned.1.call-start = ((), (), s32[]{:S(2)}) async-start(), calls=%async_computation.2 | async-start | bytes 2359296 | tf_op jit(solution)/shard_map/reduce_scatter | solution.py:36
  63.9 0.7 copy-start.2
  63.9 0.8 copy-start.3
  63.9 0.8 copy-start.1
Sparse Core Ops, SparseCore 0:
  64.0 36.5 reduce-scatter.1
